TPU v7x, 32 devices: a whole 2x2x4 slice. The times are simulated.
32 devices in a mesh: row: 8 (over z, core), col: 4 (over y, x).
Axes of the slice: x: 2, y: 2, z: 4, core: 2. Of those that a mesh axis runs over, the one named last changes fastest.
Arguments:
- inputs: bfloat16 [2, 64, 8192], P(None, None, 'col'), may hold values from -6 to 6
- w_input: bfloat16 [2, 4, 8192, 8192], P(None, None, 'row', 'col'), may hold values from -0.0625 to 0.0625
- w_recur: bfloat16 [2, 4, 8192, 8192], P(None, None, 'row', 'col'), may hold values from -0.0625 to 0.0625
- gate_bias: float32 [2, 4, 8192], P(None, None, 'row'), may hold values from -1 to 2
- hidden_init: bfloat16 [2, 64, 8192], P(None, None, ('row', 'col')), may hold values from -3 to 3
- cell_init: float32 [2, 64, 8192], P(None, None, ('row', 'col')), may hold values from -6 to 6
Outputs:
- top_hidden: bfloat16 [2, 64, 8192], P(None, None, ('row', 'col'))
- final_hidden: bfloat16 [2, 64, 8192], P(None, None, ('row', 'col'))
- final_cell: float32 [2, 64, 8192], P(None, None, ('row', 'col'))
All inputs are finite; a program needn't handle non-finite values.
Results may differ from a plain program's by a relative error of at most 0.009.
Values may be sent and summed in bfloat16 or wider, within the bound.
A program may use at most 128 MiB of HBM per device.

v0:
```python
import jax
import jax.numpy as jnp
from jax import lax
from jax.sharding import PartitionSpec as P


def lstm_cell(gate_total, cell_state):
    input_gate = jax.nn.sigmoid(gate_total[:, 0])
    forget_gate = jax.nn.sigmoid(gate_total[:, 1])
    candidate = jnp.tanh(gate_total[:, 2])
    output_gate = jax.nn.sigmoid(gate_total[:, 3])
    cell_state = forget_gate * cell_state + input_gate * candidate
    return (cell_state, (output_gate * jnp.tanh(cell_state)).astype(jnp.bfloat16))


def body(inputs, w_input, w_recur, gate_bias, hidden_init, cell_init):
    col_place = lax.axis_index("col")
    unit_width = hidden_init.shape[2]
    layers = w_input.shape[0]
    block_rows = w_input.shape[2]

    def project(vectors, weight):
        leading = vectors.shape[:-1]
        flattened = vectors.reshape(-1, vectors.shape[-1])
        result = lax.dot_general(
            flattened,
            weight.reshape(-1, weight.shape[-1]),
            (((1,), (1,)), ((), ())),
            preferred_element_type=jnp.float32,
        )
        return result.reshape(leading + (4, block_rows))

    def to_columns(owned):
        return lax.all_gather(owned, "row", axis=1, tiled=True)

    def gate_sums(partial_value, layer):
        bias_part = lax.dynamic_slice_in_dim(
            gate_bias[layer], col_place * unit_width, unit_width, 1
        )
        return (
            lax.psum_scatter(
                partial_value.astype(jnp.bfloat16), "col", scatter_dimension=2, tiled=True
            ).astype(jnp.float32)
            + bias_part[None]
        )

    def step_terms(layer, step_item):
        return project(step_item, w_input[layer])

    def advance(layer, lower_part, columns, cell_state):
        partial_value = lower_part + project(columns, w_recur[layer])
        cell_state, hidden = lstm_cell(gate_sums(partial_value, layer), cell_state)
        return (hidden, to_columns(hidden), cell_state)

    start_columns = tuple((to_columns(hidden_init[layer]) for layer in range(layers)))
    start_owned = tuple((hidden_init[layer] for layer in range(layers)))
    start_state = tuple((cell_init[layer] for layer in range(layers)))

    def advance_time(carried, step_item):
        owned_all, columns_all, cells_all = carried
        next_owned, next_columns, next_cells = ([], [], [])
        lower_part = step_terms(0, step_item)
        for layer in range(layers):
            if layer > 0:
                lower_part = project(next_columns[layer - 1], w_input[layer])
            owned, columns, cell_state = advance(
                layer, lower_part, columns_all[layer], cells_all[layer]
            )
            next_owned.append(owned)
            next_columns.append(columns)
            next_cells.append(cell_state)
        return ((tuple(next_owned), tuple(next_columns), tuple(next_cells)), next_owned[-1])

    carried, top_hidden = lax.scan(advance_time, (start_owned, start_columns, start_state), inputs)
    final_owned, final_columns, final_cells = carried
    final_hidden = jnp.stack(final_owned)
    final_cell = jnp.stack(final_cells)
    return (top_hidden, final_hidden, final_cell)


def solution(mesh):
    in_specs = (
        P(None, None, "col"),
        P(None, None, "row", "col"),
        P(None, None, "row", "col"),
        P(None, None, "row"),
        P(None, None, ("row", "col")),
        P(None, None, ("row", "col")),
    )
    out_specs = (
        P(None, None, ("row", "col")),
        P(None, None, ("row", "col")),
        P(None, None, ("row", "col")),
    )
    return jax.shard_map(body, mesh=mesh, in_specs=in_specs, out_specs=out_specs, check_vma=False)
```

profile of v0, /device:TPU:0, one launch (start us, length us, event | category | flops | bytes accessed | tf_op | source)
XLA Modules:
  0.0 273.1 jit_solution(4128591278328970384)
XLA Ops:
  7.2 0.7 fusion.68
  7.9 1.4 fusion.67
  9.3 15.9 %all-gather = bf16[1,64,2048]{2,1,0:T(8,128)(2,1)S(1)} all-gather(bf16[1,64,256]{2,1,0:T(8,128)(2,1)S(1)} %get-tuple-element.197), channel_id=2, replica_groups=mesh['row'=8,'col'=4] {'row'}, dimensions={2}, use_global_device_ids=true | all-gather | bytes 294912 | tf_op jit(solution)/shard_map/all_gather | solution.py:34
  25.2 14.2 %all-gather.1 = bf16[1,64,2048]{2,1,0:T(8,128)(2,1)S(1)} all-gather(bf16[1,64,256]{2,1,0:T(8,128)(2,1)S(1)} %get-tuple-element.194), channel_id=3, replica_groups=mesh['row'=8,'col'=4] {'row'}, dimensions={2}, use_global_device_ids=true | all-gather | bytes 294912 | tf_op jit(solution)/shard_map/all_gather | solution.py:34
  39.4 0.9 slice_bitcast_fusion
  40.3 224.2 %while.24 = (s32[]{:T(128)}, bf16[64,256]{1,0:T(8,128)(2,1)}, bf16[64,256]{1,0:T(8,128)(2,1)}, bf16[64,2048]{1,0:T(8,128)(2,1)S(1)}, bf16[64,2048]{1,0:T(8,128)(...) while((s32[]{:T(128)}, bf16[64,256]{1,0:T(8,128)(2,1)}, ...), condition=%wide.region_3.4_spmd, body=%wide.region_0.3_spmd.sunk | while | flops 4296736768 | bytes 79864096 | solution.py:74
  40.4 8.7 %fusion.90 = f32[64,4,1024]{2,0,1:T(8,128)S(1)} fusion(bf16[2,4,1024,2048]{3,2,1,0:T(8,128)(2,1)} %get-tuple-element.325, bf16[64,2048]{1,0:T(8,128)(2,1)S(1)} %get-tuple-element.304), kind=kOutput, calls=%fused_computation.4.clone.1 | convolution fusion | flops 1073741824 | bytes 18087936 | tf_op jit(solution)/shard_map/while/body/eval_jaxpr/dot_general | solution.py:25
  49.1 11.9 %fusion.91 = bf16[64,4,1024]{2,0,1:T(8,128)(2,1)} fusion(f32[64,4,1024]{2,0,1:T(8,128)S(1)} %fusion.90, bf16[2,4,1024,2048]{3,2,1,0:T(8,128)(2,1)} %get-tuple-element.324, bf16[2,64,2048]{2,1,0:T(8,128)(2,1)} %get-tuple-element.323, s32[]{:T(128)S(6)} %copy.18), kind=kOutput, calls=%fused_computation.15.clone.1 | convolution fusion | flops 1074266112 | bytes 18612228 | tf_op jit(solution)/shard_map/while/body/eval_jaxpr/dot_general | solution.py:25
  61.1 8.7 %fusion.93 = f32[64,4,1024]{2,0,1:T(8,128)S(1)} fusion(bf16[2,4,1024,2048]{3,2,1,0:T(8,128)(2,1)} %get-tuple-element.325, bf16[64,2048]{1,0:T(8,128)(2,1)S(1)} %get-tuple-element.305), kind=kOutput, calls=%fused_computation.clone.1 | convolution fusion | flops 1073741824 | bytes 18087936 | tf_op jit(solution)/shard_map/while/body/eval_jaxpr/dot_general | solution.py:25
  69.8 17.6 %reduce-scatter.3.cloned.1.call-done = bf16[64,4,256]{2,0,1:T(8,128)(2,1)} async-done(((bf16[64,4,1024]{2,0,1:T(8,128)(2,1)}), bf16[64,4,256]{2,0,1:T(8,128)(2,1)}) %reduce-scatter.3.cloned.1.call-update) | async-done | bytes 131088 | tf_op jit(solution)/shard_map/while/body/eval_jaxpr/reduce_scatter | solution.py:41
  87.4 0.9 convert_add_fusion.4
  88.3 0.1 fusion.92
  88.4 14.3 %all_gather.20 = bf16[64,2048]{1,0:T(8,128)(2,1)S(1)} all-gather(bf16[64,256]{1,0:T(8,128)(2,1)S(1)} %get-tuple-element.316), channel_id=1, replica_groups=mesh['row'=8,'col'=4] {'row'}, dimensions={1}, use_global_device_ids=true | all-gather | bytes 294912 | tf_op jit(solution)/shard_map/while/body/eval_jaxpr/all_gather | solution.py:34
  102.7 9.7 %fusion.94 = bf16[64,4,1024]{2,0,1:T(8,128)(2,1)} fusion(f32[64,4,1024]{2,0,1:T(8,128)S(1)} %fusion.93, bf16[2,4,1024,2048]{3,2,1,0:T(8,128)(2,1)} %get-tuple-element.324, bf16[64,2048]{1,0:T(8,128)(2,1)S(1)} %all_gather.20), kind=kOutput, calls=%fused_computation.14.clone.1 | convolution fusion | flops 1074266112 | bytes 18612224 | tf_op jit(solution)/shard_map/while/body/eval_jaxpr/dot_general | solution.py:25
  112.4 25.2 %reduce-scatter.5.cloned.1.call-done = bf16[64,4,256]{2,0,1:T(8,128)(2,1)} async-done(((bf16[64,4,1024]{2,0,1:T(8,128)(2,1)}), bf16[64,4,256]{2,0,1:T(8,128)(2,1)}) %reduce-scatter.5.cloned.1.call-update) | async-done | bytes 131088 | tf_op jit(solution)/shard_map/while/body/eval_jaxpr/reduce_scatter | solution.py:41
  137.6 0.9 convert_add_fusion.5
  138.6 0.1 bitcast_dynamic-update-slice_fusion.2
  138.7 14.3 %all_gather.21 = bf16[64,2048]{1,0:T(8,128)(2,1)S(1)} all-gather(bf16[64,256]{1,0:T(8,128)(2,1)S(1)} %get-tuple-element.317), channel_id=1, replica_groups=mesh['row'=8,'col'=4] {'row'}, dimensions={1}, use_global_device_ids=true | all-gather | bytes 294912 | tf_op jit(solution)/shard_map/while/body/eval_jaxpr/all_gather | solution.py:34
  153.0 8.7 %fusion.90 = f32[64,4,1024]{2,0,1:T(8,128)S(1)} fusion(bf16[2,4,1024,2048]{3,2,1,0:T(8,128)(2,1)} %get-tuple-element.325, bf16[64,2048]{1,0:T(8,128)(2,1)S(1)} %get-tuple-element.304), kind=kOutput, calls=%fused_computation.4.clone.1 | convolution fusion | flops 1073741824 | bytes 18087936 | tf_op jit(solution)/shard_map/while/body/eval_jaxpr/dot_general | solution.py:25
  161.7 11.9 %fusion.91 = bf16[64,4,1024]{2,0,1:T(8,128)(2,1)} fusion(f32[64,4,1024]{2,0,1:T(8,128)S(1)} %fusion.90, bf16[2,4,1024,2048]{3,2,1,0:T(8,128)(2,1)} %get-tuple-element.324, bf16[2,64,2048]{2,1,0:T(8,128)(2,1)} %get-tuple-element.323, s32[]{:T(128)S(6)} %copy.18), kind=kOutput, calls=%fused_computation.15.clone.1 | convolution fusion | flops 1074266112 | bytes 18612228 | tf_op jit(solution)/shard_map/while/body/eval_jaxpr/dot_general | solution.py:25
  173.7 8.7 %fusion.93 = f32[64,4,1024]{2,0,1:T(8,128)S(1)} fusion(bf16[2,4,1024,2048]{3,2,1,0:T(8,128)(2,1)} %get-tuple-element.325, bf16[64,2048]{1,0:T(8,128)(2,1)S(1)} %get-tuple-element.305), kind=kOutput, calls=%fused_computation.clone.1 | convolution fusion | flops 1073741824 | bytes 18087936 | tf_op jit(solution)/shard_map/while/body/eval_jaxpr/dot_general | solution.py:25
  182.4 16.5 %reduce-scatter.3.cloned.1.call-done = bf16[64,4,256]{2,0,1:T(8,128)(2,1)} async-done(((bf16[64,4,1024]{2,0,1:T(8,128)(2,1)}), bf16[64,4,256]{2,0,1:T(8,128)(2,1)}) %reduce-scatter.3.cloned.1.call-update) | async-done | bytes 131088 | tf_op jit(solution)/shard_map/while/body/eval_jaxpr/reduce_scatter | solution.py:41
  198.9 0.9 convert_add_fusion.4
  199.8 0.1 fusion.92
  199.9 14.3 %all_gather.20 = bf16[64,2048]{1,0:T(8,128)(2,1)S(1)} all-gather(bf16[64,256]{1,0:T(8,128)(2,1)S(1)} %get-tuple-element.316), channel_id=1, replica_groups=mesh['row'=8,'col'=4] {'row'}, dimensions={1}, use_global_device_ids=true | all-gather | bytes 294912 | tf_op jit(solution)/shard_map/while/body/eval_jaxpr/all_gather | solution.py:34
  214.2 9.7 %fusion.94 = bf16[64,4,1024]{2,0,1:T(8,128)(2,1)} fusion(f32[64,4,1024]{2,0,1:T(8,128)S(1)} %fusion.93, bf16[2,4,1024,2048]{3,2,1,0:T(8,128)(2,1)} %get-tuple-element.324, bf16[64,2048]{1,0:T(8,128)(2,1)S(1)} %all_gather.20), kind=kOutput, calls=%fused_computation.14.clone.1 | convolution fusion | flops 1074266112 | bytes 18612224 | tf_op jit(solution)/shard_map/while/body/eval_jaxpr/dot_general | solution.py:25
  223.9 25.3 %reduce-scatter.5.cloned.1.call-done = bf16[64,4,256]{2,0,1:T(8,128)(2,1)} async-done(((bf16[64,4,1024]{2,0,1:T(8,128)(2,1)}), bf16[64,4,256]{2,0,1:T(8,128)(2,1)}) %reduce-scatter.5.cloned.1.call-update) | async-done | bytes 131088 | tf_op jit(solution)/shard_map/while/body/eval_jaxpr/reduce_scatter | solution.py:41
  249.1 0.9 convert_add_fusion.5
  250.1 0.1 bitcast_dynamic-update-slice_fusion.2
  250.2 14.3 %all_gather.21 = bf16[64,2048]{1,0:T(8,128)(2,1)S(1)} all-gather(bf16[64,256]{1,0:T(8,128)(2,1)S(1)} %get-tuple-element.317), channel_id=1, replica_groups=mesh['row'=8,'col'=4] {'row'}, dimensions={1}, use_global_device_ids=true | all-gather | bytes 294912 | tf_op jit(solution)/shard_map/while/body/eval_jaxpr/all_gather | solution.py:34
  264.5 0.7 pad_maximum_fusion
  265.2 1.4 pad_maximum_fusion.1
  (20 shorter events, 0.2 us)
Async XLA Ops:
  40.3 47.1 %reduce-scatter.3.cloned.1.call-start = ((), (), s32[]{:S(2)}) async-start(), calls=%async_computation.2 | async-start | bytes 655360 | tf_op jit(solution)/shard_map/while/body/eval_jaxpr/reduce_scatter | solution.py:41
  61.0 76.6 %reduce-scatter.5.cloned.1.call-start = ((), (), s32[]{:S(2)}) async-start(), calls=%async_computation.3 | async-start | bytes 655360 | tf_op jit(solution)/shard_map/while/body/eval_jaxpr/reduce_scatter | solution.py:41
  88.4 64.6 %copy-start = (bf16[64,256]{1,0:T(8,128)(2,1)}, bf16[64,256]{1,0:T(8,128)(2,1)S(1)}, u32[]{:S(2)}) copy-start(bf16[64,256]{1,0:T(8,128)(2,1)S(1)} %get-tuple-element.316) | copy-start | bytes 98308 | tf_op jit(solution)/shard_map/while
  138.6 14.3 %copy-start.1 = (bf16[64,256]{1,0:T(8,128)(2,1)}, bf16[64,256]{1,0:T(8,128)(2,1)S(1)}, u32[]{:S(2)}) copy-start(bf16[64,256]{1,0:T(8,128)(2,1)S(1)} %get-tuple-element.317) | copy-start | bytes 98308 | tf_op jit(solution)/shard_map/while
  153.0 45.9 %reduce-scatter.3.cloned.1.call-start = ((), (), s32[]{:S(2)}) async-start(), calls=%async_computation.2 | async-start | bytes 655360 | tf_op jit(solution)/shard_map/while/body/eval_jaxpr/reduce_scatter | solution.py:41
  173.6 75.5 %reduce-scatter.5.cloned.1.call-start = ((), (), s32[]{:S(2)}) async-start(), calls=%async_computation.3 | async-start | bytes 655360 | tf_op jit(solution)/shard_map/while/body/eval_jaxpr/reduce_scatter | solution.py:41
  199.9 64.6 %copy-start = (bf16[64,256]{1,0:T(8,128)(2,1)}, bf16[64,256]{1,0:T(8,128)(2,1)S(1)}, u32[]{:S(2)}) copy-start(bf16[64,256]{1,0:T(8,128)(2,1)S(1)} %get-tuple-element.316) | copy-start | bytes 98308 | tf_op jit(solution)/shard_map/while
  250.2 14.3 %copy-start.1 = (bf16[64,256]{1,0:T(8,128)(2,1)}, bf16[64,256]{1,0:T(8,128)(2,1)S(1)}, u32[]{:S(2)}) copy-start(bf16[64,256]{1,0:T(8,128)(2,1)S(1)} %get-tuple-element.317) | copy-start | bytes 98308 | tf_op jit(solution)/shard_map/while
  264.5 2.1 copy-start.2
Sparse Core Ops, SparseCore 0:
  61.1 26.2 reduce-scatter.2
  112.6 25.0 reduce-scatter.4
  173.7 25.0 reduce-scatter.2
  224.0 25.1 reduce-scatter.4
where the time goes:
time: 274 us; the launch traced here: 273 us
  blocking collectives  87.3 us (32%)
  waiting for transfers between devices  84.6 us (31%)
  matrix products  78.1 us (29%)
  between operations  13.7 us (5%)
  other arithmetic  6.13 us (2%)
  local copies, waits for them, and re-layouts  3.06 us (1%)
    all_gather x6, blocking collectives, to_columns(): return lax.all_gather(owned, 'row', axis=1, tiled=True)  87.3 us
    reduce_scatter x4, waiting for transfers between devices, gate_sums(): lax.psum_scatter(partial_value.astype(jnp.bfloat16), 'col', scatter_dimen...  84.5 us
    dot_general x8, matrix products, project(): lax.dot_general(flattened, weight.reshape(-1, weight.shape[-1]), (((1,),...  78.1 us
  transfers between devices with their start and end apart: 4, of which 4 were waited for; matrix products, arithmetic and copies ran while one was open for 6% of the time, Pallas kernels for 0%

commit v1 on v0

--- a/solution.py
+++ b/solution.py
@@ -2,6 +2,19 @@
 import jax.numpy as jnp
 from jax import lax
 from jax.sharding import PartitionSpec as P
+
+
+def gather_around(value, axis, dim):
+    ways = lax.axis_size(axis)
+    up = [(d, (d + 1) % ways) for d in range(ways)]
+    down = [(d, (d - 1) % ways) for d in range(ways)]
+    earlier, later = ([value], [value])
+    for _ in range(ways // 2):
+        earlier.append(lax.ppermute(earlier[-1], axis, up))
+    for _ in range((ways - 1) // 2):
+        later.append(lax.ppermute(later[-1], axis, down))
+    line = jnp.concatenate([*earlier[::-1], *later[1:]], axis=dim)
+    return jnp.roll(line, (lax.axis_index(axis) - ways // 2) * value.shape[dim], axis=dim)
 
 
 def lstm_cell(gate_total, cell_state):
@@ -31,7 +44,7 @@
         return result.reshape(leading + (4, block_rows))
 
     def to_columns(owned):
-        return lax.all_gather(owned, "row", axis=1, tiled=True)
+        return gather_around(owned, "row", 1)
 
     def gate_sums(partial_value, layer):
         bias_part = lax.dynamic_slice_in_dim(

time: 274 us -> 313 us (1.14)
  blocking collectives: 87.3 us -> 0 us
  waiting for transfers between devices: 84.6 us -> 152 us
  starting transfers between devices: 0.13 us -> 57.2 us
    all_gather x6 -> x0, blocking collectives: 87.3 us -> none  [to_columns(): return lax.all_gather(owned, 'row', axis=1, tiled=True)]
    ppermute x0 -> x42, starting transfers between devices: none -> 57.1 us  [the longest x18 52.7 us: gather_around(): later.append(lax.ppermute(later[-1], axis, down))]
    ppermute x0 -> x42, waiting for transfers between devices: none -> 52 us  [the longest x24 48.3 us: gather_around(): earlier.append(lax.ppermute(earlier[-1], axis, up))]
    reduce_scatter x4, waiting for transfers between devices: 84.5 us -> 100 us  [gate_sums(): lax.psum_scatter(partial_value.astype(jnp.bfloat16), 'col', scatter_dimen...]
  transfers between devices with their start and end apart: 4 -> 46, of which waited for: 4 -> 26; matrix products, arithmetic and copies ran while one was open for 6% -> 6% of each run, Pallas kernels for 0% -> 0%
where the time goes in v1:
time: 313 us; the launch traced here: 312 us
  waiting for transfers between devices  152 us (49%)
  matrix products  78 us (25%)
  starting transfers between devices  57.2 us (18%)
  between operations  13.9 us (4%)
  other arithmetic  7.04 us (2%)
  local copies, waits for them, and re-layouts  3.41 us (1%)
    reduce_scatter x4, waiting for transfers between devices, gate_sums(): lax.psum_scatter(partial_value.astype(jnp.bfloat16), 'col', scatter_dimen...  100 us
    dot_general x8, matrix products, project(): lax.dot_general(flattened, weight.reshape(-1, weight.shape[-1]), (((1,),...  78 us
    ppermute x18, starting transfers between devices, gather_around(): later.append(lax.ppermute(later[-1], axis, down))  52.7 us
    ppermute x24, waiting for transfers between devices, gather_around(): earlier.append(lax.ppermute(earlier[-1], axis, up))  48.3 us
  transfers between devices with their start and end apart: 46, of which 26 were waited for; matrix products, arithmetic and copies ran while one was open for 6% of the time, Pallas kernels for 0%

profile of v1, /device:TPU:0, one launch (start us, length us, event | category | flops | bytes accessed | tf_op | source)
XLA Modules:
  0.0 312.4 jit_solution(4672948864040450634)
XLA Ops:
  15.5 3.8 %collective-permute-done.15 = bf16[64,256]{1,0:T(8,128)(2,1)S(1)} collective-permute-done((bf16[64,256]{1,0:T(8,128)(2,1)S(1)}, bf16[64,256]{1,0:T(8,128)(2,1)S(1)}, u32[]{:S(2)}, u32[]{:S(2)}) %collective-permute-start.15) | collective-permute-done | bytes 32800 | tf_op jit(solution)/shard_map/ppermute | solution.py:13
  25.3 3.7 %collective-permute-start.27 = (bf16[64,256]{1,0:T(8,128)(2,1)S(1)}, bf16[64,256]{1,0:T(8,128)(2,1)S(1)}, u32[]{:S(2)}, u32[]{:S(2)}) collective-permute-start(bf16[64,256]{1,0:T(8,128)(2,1)S(1)} %collective-permute-done.26), channel_id=1, source_target_pairs={{0,28},{4,0},{8,4},{12,8},{16,12},{20,16},{24,20},{28,24},{1,29},{... | collective-permute-start | bytes 98312 | tf_op jit(solution)/shard_map/ppermute | solution.py:15
  30.2 4.6 %collective-permute-done.24 = bf16[64,256]{1,0:T(8,128)(2,1)S(1)} collective-permute-done((bf16[64,256]{1,0:T(8,128)(2,1)S(1)}, bf16[64,256]{1,0:T(8,128)(2,1)S(1)}, u32[]{:S(2)}, u32[]{:S(2)}) %collective-permute-start.24) | collective-permute-done | bytes 32800 | tf_op jit(solution)/shard_map/ppermute | solution.py:13
  36.1 267.7 %while.24 = (s32[]{:T(128)}, bf16[64,256]{1,0:T(8,128)(2,1)}, bf16[64,256]{1,0:T(8,128)(2,1)}, bf16[64,2048]{1,0:T(8,128)(2,1)S(1)}, bf16[64,2048]{1,0:T(8,128)(...) while((s32[]{:T(128)}, bf16[64,256]{1,0:T(8,128)(2,1)}, ...), condition=%wide.region_3.5_spmd, body=%wide.region_0.4_spmd.sunk | while | flops 4297785344 | bytes 83207752 | solution.py:87
  36.1 8.7 %fusion.95 = f32[64,4,1024]{2,0,1:T(8,128)S(1)} fusion(bf16[2,4,1024,2048]{3,2,1,0:T(8,128)(2,1)} %get-tuple-element.354, bf16[64,2048]{1,0:T(8,128)(2,1)S(1)} %get-tuple-element.325), kind=kOutput, calls=%fused_computation.4.clone.1 | convolution fusion | flops 1073741824 | bytes 18087936 | tf_op jit(solution)/shard_map/while/body/eval_jaxpr/dot_general | solution.py:38
  44.9 11.9 %fusion.96 = bf16[64,4,1024]{2,0,1:T(8,128)(2,1)} fusion(f32[64,4,1024]{2,0,1:T(8,128)S(1)} %fusion.95, bf16[2,4,1024,2048]{3,2,1,0:T(8,128)(2,1)} %get-tuple-element.353, bf16[2,64,2048]{2,1,0:T(8,128)(2,1)} %get-tuple-element.352, s32[]{:T(128)} %get-tuple-element.322), kind=kOutput, calls=%fused_computation.15.clone.1 | convolution fusion | flops 1074266112 | bytes 18612736 | tf_op jit(solution)/shard_map/while/body/eval_jaxpr/dot_general | solution.py:38
  56.8 24.0 %reduce-scatter.3.cloned.1.call-done = bf16[64,4,256]{2,0,1:T(8,128)(2,1)} async-done(((bf16[64,4,1024]{2,0,1:T(8,128)(2,1)}), bf16[64,4,256]{2,0,1:T(8,128)(2,1)}) %reduce-scatter.3.cloned.1.call-update) | async-done | bytes 131088 | tf_op jit(solution)/shard_map/while/body/eval_jaxpr/reduce_scatter | solution.py:54
  81.9 5.1 %collective-permute-done = bf16[64,256]{1,0:T(8,128)(2,1)S(1)} collective-permute-done((bf16[64,256]{1,0:T(8,128)(2,1)S(1)}, bf16[64,256]{1,0:T(8,128)(2,1)S(1)}, u32[]{:S(2)}, u32[]{:S(2)}) %collective-permute-start) | collective-permute-done | bytes 32800 | tf_op jit(solution)/shard_map/while/body/eval_jaxpr/ppermute | solution.py:13
  87.0 3.5 %collective-permute-start.4 = (bf16[64,256]{1,0:T(8,128)(2,1)S(1)}, bf16[64,256]{1,0:T(8,128)(2,1)S(1)}, u32[]{:S(2)}, u32[]{:S(2)}) collective-permute-start(bf16[64,256]{1,0:T(8,128)(2,1)S(1)} %get-tuple-element.345), channel_id=1, source_target_pairs={{0,28},{4,0},{8,4},{12,8},{16,12},{20,16},{24,20},{28,24},{1,29},{... | collective-permute-start | bytes 98312 | tf_op jit(solution)/shard_map/while/body/eval_jaxpr/ppermute | solution.py:15
  92.5 3.5 %collective-permute-start.5 = (bf16[64,256]{1,0:T(8,128)(2,1)S(1)}, bf16[64,256]{1,0:T(8,128)(2,1)S(1)}, u32[]{:S(2)}, u32[]{:S(2)}) collective-permute-start(bf16[64,256]{1,0:T(8,128)(2,1)S(1)} %collective-permute-done.4), channel_id=1, source_target_pairs={{0,28},{4,0},{8,4},{12,8},{16,12},{20,16},{24,20},{28,24},{1,29},{... | collective-permute-start | bytes 98312 | tf_op jit(solution)/shard_map/while/body/eval_jaxpr/ppermute | solution.py:15
  97.6 8.7 %fusion.98 = f32[64,4,1024]{2,0,1:T(8,128)S(1)} fusion(bf16[2,4,1024,2048]{3,2,1,0:T(8,128)(2,1)} %get-tuple-element.354, bf16[64,2048]{1,0:T(8,128)(2,1)S(1)} %get-tuple-element.326), kind=kOutput, calls=%fused_computation.clone.1 | convolution fusion | flops 1073741824 | bytes 18087936 | tf_op jit(solution)/shard_map/while/body/eval_jaxpr/dot_general | solution.py:38
  106.4 3.6 %collective-permute-start.6 = (bf16[64,256]{1,0:T(8,128)(2,1)S(1)}, bf16[64,256]{1,0:T(8,128)(2,1)S(1)}, u32[]{:S(2)}, u32[]{:S(2)}) collective-permute-start(bf16[64,256]{1,0:T(8,128)(2,1)S(1)} %collective-permute-done.5), channel_id=1, source_target_pairs={{0,28},{4,0},{8,4},{12,8},{16,12},{20,16},{24,20},{28,24},{1,29},{... | collective-permute-start | bytes 98312 | tf_op jit(solution)/shard_map/while/body/eval_jaxpr/ppermute | solution.py:15
  111.7 9.7 %fusion.100 = bf16[64,4,1024]{2,0,1:T(8,128)(2,1)} fusion(f32[64,4,1024]{2,0,1:T(8,128)S(1)} %fusion.98, bf16[2,4,1024,2048]{3,2,1,0:T(8,128)(2,1)} %get-tuple-element.353, bf16[64,2048]{1,0:T(8,128)(2,1)S(1)} %fusion.99), kind=kOutput, calls=%fused_computation.14.clone.1 | convolution fusion | flops 1074266112 | bytes 18612224 | tf_op jit(solution)/shard_map/while/body/eval_jaxpr/dot_general | solution.py:38
  121.4 25.5 %reduce-scatter.5.cloned.1.call-done = bf16[64,4,256]{2,0,1:T(8,128)(2,1)} async-done(((bf16[64,4,1024]{2,0,1:T(8,128)(2,1)}), bf16[64,4,256]{2,0,1:T(8,128)(2,1)}) %reduce-scatter.5.cloned.1.call-update) | async-done | bytes 131088 | tf_op jit(solution)/shard_map/while/body/eval_jaxpr/reduce_scatter | solution.py:54
  148.0 5.1 %collective-permute-done.7 = bf16[64,256]{1,0:T(8,128)(2,1)S(1)} collective-permute-done((bf16[64,256]{1,0:T(8,128)(2,1)S(1)}, bf16[64,256]{1,0:T(8,128)(2,1)S(1)}, u32[]{:S(2)}, u32[]{:S(2)}) %collective-permute-start.7) | collective-permute-done | bytes 32800 | tf_op jit(solution)/shard_map/while/body/eval_jaxpr/ppermute | solution.py:13
  153.1 3.5 %collective-permute-start.11 = (bf16[64,256]{1,0:T(8,128)(2,1)S(1)}, bf16[64,256]{1,0:T(8,128)(2,1)S(1)}, u32[]{:S(2)}, u32[]{:S(2)}) collective-permute-start(bf16[64,256]{1,0:T(8,128)(2,1)S(1)} %get-tuple-element.346), channel_id=1, source_target_pairs={{0,28},{4,0},{8,4},{12,8},{16,12},{20,16},{24,20},{28,24},{1,29},{... | collective-permute-start | bytes 98312 | tf_op jit(solution)/shard_map/while/body/eval_jaxpr/ppermute | solution.py:15
  158.6 3.5 %collective-permute-start.12 = (bf16[64,256]{1,0:T(8,128)(2,1)S(1)}, bf16[64,256]{1,0:T(8,128)(2,1)S(1)}, u32[]{:S(2)}, u32[]{:S(2)}) collective-permute-start(bf16[64,256]{1,0:T(8,128)(2,1)S(1)} %collective-permute-done.11), channel_id=1, source_target_pairs={{0,28},{4,0},{8,4},{12,8},{16,12},{20,16},{24,20},{28,24},{1,29},{... | collective-permute-start | bytes 98312 | tf_op jit(solution)/shard_map/while/body/eval_jaxpr/ppermute | solution.py:15
  163.9 3.5 %collective-permute-start.13 = (bf16[64,256]{1,0:T(8,128)(2,1)S(1)}, bf16[64,256]{1,0:T(8,128)(2,1)S(1)}, u32[]{:S(2)}, u32[]{:S(2)}) collective-permute-start(bf16[64,256]{1,0:T(8,128)(2,1)S(1)} %collective-permute-done.12), channel_id=1, source_target_pairs={{0,28},{4,0},{8,4},{12,8},{16,12},{20,16},{24,20},{28,24},{1,29},{... | collective-permute-start | bytes 98312 | tf_op jit(solution)/shard_map/while/body/eval_jaxpr/ppermute | solution.py:15
  169.3 8.7 %fusion.95 = f32[64,4,1024]{2,0,1:T(8,128)S(1)} fusion(bf16[2,4,1024,2048]{3,2,1,0:T(8,128)(2,1)} %get-tuple-element.354, bf16[64,2048]{1,0:T(8,128)(2,1)S(1)} %get-tuple-element.325), kind=kOutput, calls=%fused_computation.4.clone.1 | convolution fusion | flops 1073741824 | bytes 18087936 | tf_op jit(solution)/shard_map/while/body/eval_jaxpr/dot_general | solution.py:38
  178.1 11.9 %fusion.96 = bf16[64,4,1024]{2,0,1:T(8,128)(2,1)} fusion(f32[64,4,1024]{2,0,1:T(8,128)S(1)} %fusion.95, bf16[2,4,1024,2048]{3,2,1,0:T(8,128)(2,1)} %get-tuple-element.353, bf16[2,64,2048]{2,1,0:T(8,128)(2,1)} %get-tuple-element.352, s32[]{:T(128)} %get-tuple-element.322), kind=kOutput, calls=%fused_computation.15.clone.1 | convolution fusion | flops 1074266112 | bytes 18612736 | tf_op jit(solution)/shard_map/while/body/eval_jaxpr/dot_general | solution.py:38
  190.0 25.3 %reduce-scatter.3.cloned.1.call-done = bf16[64,4,256]{2,0,1:T(8,128)(2,1)} async-done(((bf16[64,4,1024]{2,0,1:T(8,128)(2,1)}), bf16[64,4,256]{2,0,1:T(8,128)(2,1)}) %reduce-scatter.3.cloned.1.call-update) | async-done | bytes 131088 | tf_op jit(solution)/shard_map/while/body/eval_jaxpr/reduce_scatter | solution.py:54
  216.4 5.1 %collective-permute-done = bf16[64,256]{1,0:T(8,128)(2,1)S(1)} collective-permute-done((bf16[64,256]{1,0:T(8,128)(2,1)S(1)}, bf16[64,256]{1,0:T(8,128)(2,1)S(1)}, u32[]{:S(2)}, u32[]{:S(2)}) %collective-permute-start) | collective-permute-done | bytes 32800 | tf_op jit(solution)/shard_map/while/body/eval_jaxpr/ppermute | solution.py:13
  221.5 3.5 %collective-permute-start.4 = (bf16[64,256]{1,0:T(8,128)(2,1)S(1)}, bf16[64,256]{1,0:T(8,128)(2,1)S(1)}, u32[]{:S(2)}, u32[]{:S(2)}) collective-permute-start(bf16[64,256]{1,0:T(8,128)(2,1)S(1)} %get-tuple-element.345), channel_id=1, source_target_pairs={{0,28},{4,0},{8,4},{12,8},{16,12},{20,16},{24,20},{28,24},{1,29},{... | collective-permute-start | bytes 98312 | tf_op jit(solution)/shard_map/while/body/eval_jaxpr/ppermute | solution.py:15
  227.0 3.5 %collective-permute-start.5 = (bf16[64,256]{1,0:T(8,128)(2,1)S(1)}, bf16[64,256]{1,0:T(8,128)(2,1)S(1)}, u32[]{:S(2)}, u32[]{:S(2)}) collective-permute-start(bf16[64,256]{1,0:T(8,128)(2,1)S(1)} %collective-permute-done.4), channel_id=1, source_target_pairs={{0,28},{4,0},{8,4},{12,8},{16,12},{20,16},{24,20},{28,24},{1,29},{... | collective-permute-start | bytes 98312 | tf_op jit(solution)/shard_map/while/body/eval_jaxpr/ppermute | solution.py:15
  232.1 8.7 %fusion.98 = f32[64,4,1024]{2,0,1:T(8,128)S(1)} fusion(bf16[2,4,1024,2048]{3,2,1,0:T(8,128)(2,1)} %get-tuple-element.354, bf16[64,2048]{1,0:T(8,128)(2,1)S(1)} %get-tuple-element.326), kind=kOutput, calls=%fused_computation.clone.1 | convolution fusion | flops 1073741824 | bytes 18087936 | tf_op jit(solution)/shard_map/while/body/eval_jaxpr/dot_general | solution.py:38
  240.9 3.6 %collective-permute-start.6 = (bf16[64,256]{1,0:T(8,128)(2,1)S(1)}, bf16[64,256]{1,0:T(8,128)(2,1)S(1)}, u32[]{:S(2)}, u32[]{:S(2)}) collective-permute-start(bf16[64,256]{1,0:T(8,128)(2,1)S(1)} %collective-permute-done.5), channel_id=1, source_target_pairs={{0,28},{4,0},{8,4},{12,8},{16,12},{20,16},{24,20},{28,24},{1,29},{... | collective-permute-start | bytes 98312 | tf_op jit(solution)/shard_map/while/body/eval_jaxpr/ppermute | solution.py:15
  246.3 9.7 %fusion.100 = bf16[64,4,1024]{2,0,1:T(8,128)(2,1)} fusion(f32[64,4,1024]{2,0,1:T(8,128)S(1)} %fusion.98, bf16[2,4,1024,2048]{3,2,1,0:T(8,128)(2,1)} %get-tuple-element.353, bf16[64,2048]{1,0:T(8,128)(2,1)S(1)} %fusion.99), kind=kOutput, calls=%fused_computation.14.clone.1 | convolution fusion | flops 1074266112 | bytes 18612224 | tf_op jit(solution)/shard_map/while/body/eval_jaxpr/dot_general | solution.py:38
  255.9 25.5 %reduce-scatter.5.cloned.1.call-done = bf16[64,4,256]{2,0,1:T(8,128)(2,1)} async-done(((bf16[64,4,1024]{2,0,1:T(8,128)(2,1)}), bf16[64,4,256]{2,0,1:T(8,128)(2,1)}) %reduce-scatter.5.cloned.1.call-update) | async-done | bytes 131088 | tf_op jit(solution)/shard_map/while/body/eval_jaxpr/reduce_scatter | solution.py:54
  282.6 5.1 %collective-permute-done.7 = bf16[64,256]{1,0:T(8,128)(2,1)S(1)} collective-permute-done((bf16[64,256]{1,0:T(8,128)(2,1)S(1)}, bf16[64,256]{1,0:T(8,128)(2,1)S(1)}, u32[]{:S(2)}, u32[]{:S(2)}) %collective-permute-start.7) | collective-permute-done | bytes 32800 | tf_op jit(solution)/shard_map/while/body/eval_jaxpr/ppermute | solution.py:13
  287.7 3.5 %collective-permute-start.11 = (bf16[64,256]{1,0:T(8,128)(2,1)S(1)}, bf16[64,256]{1,0:T(8,128)(2,1)S(1)}, u32[]{:S(2)}, u32[]{:S(2)}) collective-permute-start(bf16[64,256]{1,0:T(8,128)(2,1)S(1)} %get-tuple-element.346), channel_id=1, source_target_pairs={{0,28},{4,0},{8,4},{12,8},{16,12},{20,16},{24,20},{28,24},{1,29},{... | collective-permute-start | bytes 98312 | tf_op jit(solution)/shard_map/while/body/eval_jaxpr/ppermute | solution.py:15
  293.1 3.5 %collective-permute-start.12 = (bf16[64,256]{1,0:T(8,128)(2,1)S(1)}, bf16[64,256]{1,0:T(8,128)(2,1)S(1)}, u32[]{:S(2)}, u32[]{:S(2)}) collective-permute-start(bf16[64,256]{1,0:T(8,128)(2,1)S(1)} %collective-permute-done.11), channel_id=1, source_target_pairs={{0,28},{4,0},{8,4},{12,8},{16,12},{20,16},{24,20},{28,24},{1,29},{... | collective-permute-start | bytes 98312 | tf_op jit(solution)/shard_map/while/body/eval_jaxpr/ppermute | solution.py:15
  298.4 3.5 %collective-permute-start.13 = (bf16[64,256]{1,0:T(8,128)(2,1)S(1)}, bf16[64,256]{1,0:T(8,128)(2,1)S(1)}, u32[]{:S(2)}, u32[]{:S(2)}) collective-permute-start(bf16[64,256]{1,0:T(8,128)(2,1)S(1)} %collective-permute-done.12), channel_id=1, source_target_pairs={{0,28},{4,0},{8,4},{12,8},{16,12},{20,16},{24,20},{28,24},{1,29},{... | collective-permute-start | bytes 98312 | tf_op jit(solution)/shard_map/while/body/eval_jaxpr/ppermute | solution.py:15
  (155 shorter events, 44.5 us)
Async XLA Ops:
  8.0 6.2 %collective-permute-start.14 = (bf16[64,256]{1,0:T(8,128)(2,1)S(1)}, bf16[64,256]{1,0:T(8,128)(2,1)S(1)}, u32[]{:S(2)}, u32[]{:S(2)}) collective-permute-start(bf16[64,256]{1,0:T(8,128)(2,1)S(1)} %get-tuple-element.301), channel_id=1, source_target_pairs={{0,4},{4,8},{8,12},{12,16},{16,20},{20,24},{24,28},{28,0},{1,5},{5... | collective-permute-start | bytes 98312 | tf_op jit(solution)/shard_map/ppermute | solution.py:13
  8.5 6.5 %collective-permute-start.21 = (bf16[64,256]{1,0:T(8,128)(2,1)S(1)}, bf16[64,256]{1,0:T(8,128)(2,1)S(1)}, u32[]{:S(2)}, u32[]{:S(2)}) collective-permute-start(bf16[64,256]{1,0:T(8,128)(2,1)S(1)} %get-tuple-element.302), channel_id=1, source_target_pairs={{0,4},{4,8},{8,12},{12,16},{16,20},{20,24},{24,28},{28,0},{1,5},{5... | collective-permute-start | bytes 98312 | tf_op jit(solution)/shard_map/ppermute | solution.py:13
  11.2 8.8 %collective-permute-start.25 = (bf16[64,256]{1,0:T(8,128)(2,1)S(1)}, bf16[64,256]{1,0:T(8,128)(2,1)S(1)}, u32[]{:S(2)}, u32[]{:S(2)}) collective-permute-start(bf16[64,256]{1,0:T(8,128)(2,1)S(1)} %get-tuple-element.302), channel_id=1, source_target_pairs={{0,28},{4,0},{8,4},{12,8},{16,12},{20,16},{24,20},{28,24},{1,29},{... | collective-permute-start | bytes 98312 | tf_op jit(solution)/shard_map/ppermute | solution.py:15
  12.7 10.9 %collective-permute-start.18 = (bf16[64,256]{1,0:T(8,128)(2,1)S(1)}, bf16[64,256]{1,0:T(8,128)(2,1)S(1)}, u32[]{:S(2)}, u32[]{:S(2)}) collective-permute-start(bf16[64,256]{1,0:T(8,128)(2,1)S(1)} %get-tuple-element.301), channel_id=1, source_target_pairs={{0,28},{4,0},{8,4},{12,8},{16,12},{20,16},{24,20},{28,24},{1,29},{... | collective-permute-start | bytes 98312 | tf_op jit(solution)/shard_map/ppermute | solution.py:15
  15.0 8.6 %collective-permute-start.22 = (bf16[64,256]{1,0:T(8,128)(2,1)S(1)}, bf16[64,256]{1,0:T(8,128)(2,1)S(1)}, u32[]{:S(2)}, u32[]{:S(2)}) collective-permute-start(bf16[64,256]{1,0:T(8,128)(2,1)S(1)} %collective-permute-done.21), channel_id=1, source_target_pairs={{0,4},{4,8},{8,12},{12,16},{16,20},{20,24},{24,28},{28,0},{1,5},{5... | collective-permute-start | bytes 98312 | tf_op jit(solution)/shard_map/ppermute | solution.py:13
  19.3 5.5 %collective-permute-start.16 = (bf16[64,256]{1,0:T(8,128)(2,1)S(1)}, bf16[64,256]{1,0:T(8,128)(2,1)S(1)}, u32[]{:S(2)}, u32[]{:S(2)}) collective-permute-start(bf16[64,256]{1,0:T(8,128)(2,1)S(1)} %collective-permute-done.15), channel_id=1, source_target_pairs={{0,4},{4,8},{8,12},{12,16},{16,20},{20,24},{24,28},{28,0},{1,5},{5... | collective-permute-start | bytes 98312 | tf_op jit(solution)/shard_map/ppermute | solution.py:13
  20.0 5.3 %collective-permute-start.26 = (bf16[64,256]{1,0:T(8,128)(2,1)S(1)}, bf16[64,256]{1,0:T(8,128)(2,1)S(1)}, u32[]{:S(2)}, u32[]{:S(2)}) collective-permute-start(bf16[64,256]{1,0:T(8,128)(2,1)S(1)} %collective-permute-done.25), channel_id=1, source_target_pairs={{0,28},{4,0},{8,4},{12,8},{16,12},{20,16},{24,20},{28,24},{1,29},{... | collective-permute-start | bytes 98312 | tf_op jit(solution)/shard_map/ppermute | solution.py:15
  23.6 5.5 %collective-permute-start.19 = (bf16[64,256]{1,0:T(8,128)(2,1)S(1)}, bf16[64,256]{1,0:T(8,128)(2,1)S(1)}, u32[]{:S(2)}, u32[]{:S(2)}) collective-permute-start(bf16[64,256]{1,0:T(8,128)(2,1)S(1)} %collective-permute-done.18), channel_id=1, source_target_pairs={{0,28},{4,0},{8,4},{12,8},{16,12},{20,16},{24,20},{28,24},{1,29},{... | collective-permute-start | bytes 98312 | tf_op jit(solution)/shard_map/ppermute | solution.py:15
  23.6 6.1 %collective-permute-start.23 = (bf16[64,256]{1,0:T(8,128)(2,1)S(1)}, bf16[64,256]{1,0:T(8,128)(2,1)S(1)}, u32[]{:S(2)}, u32[]{:S(2)}) collective-permute-start(bf16[64,256]{1,0:T(8,128)(2,1)S(1)} %collective-permute-done.22), channel_id=1, source_target_pairs={{0,4},{4,8},{8,12},{12,16},{16,20},{20,24},{24,28},{28,0},{1,5},{5... | collective-permute-start | bytes 98312 | tf_op jit(solution)/shard_map/ppermute | solution.py:13
  24.8 5.4 %collective-permute-start.17 = (bf16[64,256]{1,0:T(8,128)(2,1)S(1)}, bf16[64,256]{1,0:T(8,128)(2,1)S(1)}, u32[]{:S(2)}, u32[]{:S(2)}) collective-permute-start(bf16[64,256]{1,0:T(8,128)(2,1)S(1)} %collective-permute-done.16), channel_id=1, source_target_pairs={{0,4},{4,8},{8,12},{12,16},{16,20},{20,24},{24,28},{28,0},{1,5},{5... | collective-permute-start | bytes 98312 | tf_op jit(solution)/shard_map/ppermute | solution.py:13
  25.3 10.3 %collective-permute-start.27 = (bf16[64,256]{1,0:T(8,128)(2,1)S(1)}, bf16[64,256]{1,0:T(8,128)(2,1)S(1)}, u32[]{:S(2)}, u32[]{:S(2)}) collective-permute-start(bf16[64,256]{1,0:T(8,128)(2,1)S(1)} %collective-permute-done.26), channel_id=1, source_target_pairs={{0,28},{4,0},{8,4},{12,8},{16,12},{20,16},{24,20},{28,24},{1,29},{... | collective-permute-start | bytes 98312 | tf_op jit(solution)/shard_map/ppermute | solution.py:15
  29.0 6.8 %collective-permute-start.20 = (bf16[64,256]{1,0:T(8,128)(2,1)S(1)}, bf16[64,256]{1,0:T(8,128)(2,1)S(1)}, u32[]{:S(2)}, u32[]{:S(2)}) collective-permute-start(bf16[64,256]{1,0:T(8,128)(2,1)S(1)} %collective-permute-done.19), channel_id=1, source_target_pairs={{0,28},{4,0},{8,4},{12,8},{16,12},{20,16},{24,20},{28,24},{1,29},{... | collective-permute-start | bytes 98312 | tf_op jit(solution)/shard_map/ppermute | solution.py:15
  36.1 44.7 %reduce-scatter.3.cloned.1.call-start = ((), (), s32[]{:S(2)}) async-start(), calls=%async_computation.2 | async-start | bytes 655360 | tf_op jit(solution)/shard_map/while/body/eval_jaxpr/reduce_scatter | solution.py:54
  56.8 90.1 %reduce-scatter.5.cloned.1.call-start = ((), (), s32[]{:S(2)}) async-start(), calls=%async_computation.3 | async-start | bytes 655360 | tf_op jit(solution)/shard_map/while/body/eval_jaxpr/reduce_scatter | solution.py:54
  87.0 5.5 %collective-permute-start.1 = (bf16[64,256]{1,0:T(8,128)(2,1)S(1)}, bf16[64,256]{1,0:T(8,128)(2,1)S(1)}, u32[]{:S(2)}, u32[]{:S(2)}) collective-permute-start(bf16[64,256]{1,0:T(8,128)(2,1)S(1)} %collective-permute-done), channel_id=1, source_target_pairs={{0,4},{4,8},{8,12},{12,16},{16,20},{20,24},{24,28},{28,0},{1,5},{5... | collective-permute-start | bytes 98312 | tf_op jit(solution)/shard_map/while/body/eval_jaxpr/ppermute | solution.py:13
  87.0 5.5 %collective-permute-start.4 = (bf16[64,256]{1,0:T(8,128)(2,1)S(1)}, bf16[64,256]{1,0:T(8,128)(2,1)S(1)}, u32[]{:S(2)}, u32[]{:S(2)}) collective-permute-start(bf16[64,256]{1,0:T(8,128)(2,1)S(1)} %get-tuple-element.345), channel_id=1, source_target_pairs={{0,28},{4,0},{8,4},{12,8},{16,12},{20,16},{24,20},{28,24},{1,29},{... | collective-permute-start | bytes 98312 | tf_op jit(solution)/shard_map/while/body/eval_jaxpr/ppermute | solution.py:15
  92.5 13.9 %collective-permute-start.5 = (bf16[64,256]{1,0:T(8,128)(2,1)S(1)}, bf16[64,256]{1,0:T(8,128)(2,1)S(1)}, u32[]{:S(2)}, u32[]{:S(2)}) collective-permute-start(bf16[64,256]{1,0:T(8,128)(2,1)S(1)} %collective-permute-done.4), channel_id=1, source_target_pairs={{0,28},{4,0},{8,4},{12,8},{16,12},{20,16},{24,20},{28,24},{1,29},{... | collective-permute-start | bytes 98312 | tf_op jit(solution)/shard_map/while/body/eval_jaxpr/ppermute | solution.py:15
  97.6 12.4 %collective-permute-start.3 = (bf16[64,256]{1,0:T(8,128)(2,1)S(1)}, bf16[64,256]{1,0:T(8,128)(2,1)S(1)}, u32[]{:S(2)}, u32[]{:S(2)}) collective-permute-start(bf16[64,256]{1,0:T(8,128)(2,1)S(1)} %collective-permute-done.2), channel_id=1, source_target_pairs={{0,4},{4,8},{8,12},{12,16},{16,20},{20,24},{24,28},{28,0},{1,5},{5... | collective-permute-start | bytes 98312 | tf_op jit(solution)/shard_map/while/body/eval_jaxpr/ppermute | solution.py:13
  153.1 5.5 %collective-permute-start.8 = (bf16[64,256]{1,0:T(8,128)(2,1)S(1)}, bf16[64,256]{1,0:T(8,128)(2,1)S(1)}, u32[]{:S(2)}, u32[]{:S(2)}) collective-permute-start(bf16[64,256]{1,0:T(8,128)(2,1)S(1)} %collective-permute-done.7), channel_id=1, source_target_pairs={{0,4},{4,8},{8,12},{12,16},{16,20},{20,24},{24,28},{28,0},{1,5},{5... | collective-permute-start | bytes 98312 | tf_op jit(solution)/shard_map/while/body/eval_jaxpr/ppermute | solution.py:13
  153.1 5.5 %collective-permute-start.11 = (bf16[64,256]{1,0:T(8,128)(2,1)S(1)}, bf16[64,256]{1,0:T(8,128)(2,1)S(1)}, u32[]{:S(2)}, u32[]{:S(2)}) collective-permute-start(bf16[64,256]{1,0:T(8,128)(2,1)S(1)} %get-tuple-element.346), channel_id=1, source_target_pairs={{0,28},{4,0},{8,4},{12,8},{16,12},{20,16},{24,20},{28,24},{1,29},{... | collective-permute-start | bytes 98312 | tf_op jit(solution)/shard_map/while/body/eval_jaxpr/ppermute | solution.py:15
  158.6 5.2 %collective-permute-start.9 = (bf16[64,256]{1,0:T(8,128)(2,1)S(1)}, bf16[64,256]{1,0:T(8,128)(2,1)S(1)}, u32[]{:S(2)}, u32[]{:S(2)}) collective-permute-start(bf16[64,256]{1,0:T(8,128)(2,1)S(1)} %collective-permute-done.8), channel_id=1, source_target_pairs={{0,4},{4,8},{8,12},{12,16},{16,20},{20,24},{24,28},{28,0},{1,5},{5... | collective-permute-start | bytes 98312 | tf_op jit(solution)/shard_map/while/body/eval_jaxpr/ppermute | solution.py:13
  158.6 5.2 %collective-permute-start.12 = (bf16[64,256]{1,0:T(8,128)(2,1)S(1)}, bf16[64,256]{1,0:T(8,128)(2,1)S(1)}, u32[]{:S(2)}, u32[]{:S(2)}) collective-permute-start(bf16[64,256]{1,0:T(8,128)(2,1)S(1)} %collective-permute-done.11), channel_id=1, source_target_pairs={{0,28},{4,0},{8,4},{12,8},{16,12},{20,16},{24,20},{28,24},{1,29},{... | collective-permute-start | bytes 98312 | tf_op jit(solution)/shard_map/while/body/eval_jaxpr/ppermute | solution.py:15
  169.3 46.0 %reduce-scatter.3.cloned.1.call-start = ((), (), s32[]{:S(2)}) async-start(), calls=%async_computation.2 | async-start | bytes 655360 | tf_op jit(solution)/shard_map/while/body/eval_jaxpr/reduce_scatter | solution.py:54
  190.0 91.5 %reduce-scatter.5.cloned.1.call-start = ((), (), s32[]{:S(2)}) async-start(), calls=%async_computation.3 | async-start | bytes 655360 | tf_op jit(solution)/shard_map/while/body/eval_jaxpr/reduce_scatter | solution.py:54
  221.5 5.5 %collective-permute-start.1 = (bf16[64,256]{1,0:T(8,128)(2,1)S(1)}, bf16[64,256]{1,0:T(8,128)(2,1)S(1)}, u32[]{:S(2)}, u32[]{:S(2)}) collective-permute-start(bf16[64,256]{1,0:T(8,128)(2,1)S(1)} %collective-permute-done), channel_id=1, source_target_pairs={{0,4},{4,8},{8,12},{12,16},{16,20},{20,24},{24,28},{28,0},{1,5},{5... | collective-permute-start | bytes 98312 | tf_op jit(solution)/shard_map/while/body/eval_jaxpr/ppermute | solution.py:13
  221.5 5.5 %collective-permute-start.4 = (bf16[64,256]{1,0:T(8,128)(2,1)S(1)}, bf16[64,256]{1,0:T(8,128)(2,1)S(1)}, u32[]{:S(2)}, u32[]{:S(2)}) collective-permute-start(bf16[64,256]{1,0:T(8,128)(2,1)S(1)} %get-tuple-element.345), channel_id=1, source_target_pairs={{0,28},{4,0},{8,4},{12,8},{16,12},{20,16},{24,20},{28,24},{1,29},{... | collective-permute-start | bytes 98312 | tf_op jit(solution)/shard_map/while/body/eval_jaxpr/ppermute | solution.py:15
  227.0 13.9 %collective-permute-start.5 = (bf16[64,256]{1,0:T(8,128)(2,1)S(1)}, bf16[64,256]{1,0:T(8,128)(2,1)S(1)}, u32[]{:S(2)}, u32[]{:S(2)}) collective-permute-start(bf16[64,256]{1,0:T(8,128)(2,1)S(1)} %collective-permute-done.4), channel_id=1, source_target_pairs={{0,28},{4,0},{8,4},{12,8},{16,12},{20,16},{24,20},{28,24},{1,29},{... | collective-permute-start | bytes 98312 | tf_op jit(solution)/shard_map/while/body/eval_jaxpr/ppermute | solution.py:15
  232.1 12.4 %collective-permute-start.3 = (bf16[64,256]{1,0:T(8,128)(2,1)S(1)}, bf16[64,256]{1,0:T(8,128)(2,1)S(1)}, u32[]{:S(2)}, u32[]{:S(2)}) collective-permute-start(bf16[64,256]{1,0:T(8,128)(2,1)S(1)} %collective-permute-done.2), channel_id=1, source_target_pairs={{0,4},{4,8},{8,12},{12,16},{16,20},{20,24},{24,28},{28,0},{1,5},{5... | collective-permute-start | bytes 98312 | tf_op jit(solution)/shard_map/while/body/eval_jaxpr/ppermute | solution.py:13
  287.7 5.4 %collective-permute-start.8 = (bf16[64,256]{1,0:T(8,128)(2,1)S(1)}, bf16[64,256]{1,0:T(8,128)(2,1)S(1)}, u32[]{:S(2)}, u32[]{:S(2)}) collective-permute-start(bf16[64,256]{1,0:T(8,128)(2,1)S(1)} %collective-permute-done.7), channel_id=1, source_target_pairs={{0,4},{4,8},{8,12},{12,16},{16,20},{20,24},{24,28},{28,0},{1,5},{5... | collective-permute-start | bytes 98312 | tf_op jit(solution)/shard_map/while/body/eval_jaxpr/ppermute | solution.py:13
  287.7 5.4 %collective-permute-start.11 = (bf16[64,256]{1,0:T(8,128)(2,1)S(1)}, bf16[64,256]{1,0:T(8,128)(2,1)S(1)}, u32[]{:S(2)}, u32[]{:S(2)}) collective-permute-start(bf16[64,256]{1,0:T(8,128)(2,1)S(1)} %get-tuple-element.346), channel_id=1, source_target_pairs={{0,28},{4,0},{8,4},{12,8},{16,12},{20,16},{24,20},{28,24},{1,29},{... | collective-permute-start | bytes 98312 | tf_op jit(solution)/shard_map/while/body/eval_jaxpr/ppermute | solution.py:15
  293.1 5.2 %collective-permute-start.9 = (bf16[64,256]{1,0:T(8,128)(2,1)S(1)}, bf16[64,256]{1,0:T(8,128)(2,1)S(1)}, u32[]{:S(2)}, u32[]{:S(2)}) collective-permute-start(bf16[64,256]{1,0:T(8,128)(2,1)S(1)} %collective-permute-done.8), channel_id=1, source_target_pairs={{0,4},{4,8},{8,12},{12,16},{16,20},{20,24},{24,28},{28,0},{1,5},{5... | collective-permute-start | bytes 98312 | tf_op jit(solution)/shard_map/while/body/eval_jaxpr/ppermute | solution.py:13
  293.1 5.2 %collective-permute-start.12 = (bf16[64,256]{1,0:T(8,128)(2,1)S(1)}, bf16[64,256]{1,0:T(8,128)(2,1)S(1)}, u32[]{:S(2)}, u32[]{:S(2)}) collective-permute-start(bf16[64,256]{1,0:T(8,128)(2,1)S(1)} %collective-permute-done.11), channel_id=1, source_target_pairs={{0,28},{4,0},{8,4},{12,8},{16,12},{20,16},{24,20},{28,24},{1,29},{... | collective-permute-start | bytes 98312 | tf_op jit(solution)/shard_map/while/body/eval_jaxpr/ppermute | solution.py:15
  (21 other events, 348.1 us)
Sparse Core Ops, SparseCore 0:
  56.9 23.8 reduce-scatter.2
  121.6 25.3 reduce-scatter.4
  190.1 25.1 reduce-scatter.2
  256.1 25.3 reduce-scatter.4
